TPU v7x, 32 devices: a whole 2x2x4 slice. The times are simulated.
32 devices in a mesh: seq: 8 (over z, x), doc: 4 (over y, core).
Axes of the slice: x: 2, y: 2, z: 4, core: 2. Of those that a mesh axis runs over, the one named last changes fastest.
Arguments:
- tokens: bfloat16 [16, 8192, 512], P('doc', 'seq'), may hold values from -6 to 6
- factor_one: bfloat16 [8, 1024, 1024], P('seq'), may hold values from -0.1875 to 0.1875
- factor_two: bfloat16 [1024, 8, 8], P('seq'), may hold values from -2 to 2
- gate_gain: float32 [512], replicated, may hold values from 0.5 to 2
- gate_bias: float32 [512], replicated, may hold values from -4 to 4
- block_counts: int32 [16], replicated, may hold values from 7 to 8, as said below
- partner: int32 [16], replicated, may hold values from 0 to 15, as said below
- reading: float32 [512, 256], replicated, may hold values from -0.25 to 0.25
Outputs:
- gated: bfloat16 [16, 8, 1024, 512], P('doc', None, 'seq')
- contrast: float32 [16, 256], P('doc')
Inputs may be any that keep to these rules, and one draw needn't show every extreme that they name: `block_counts`: some document has all 8 blocks valid and another exactly 7. partner is a single cycle through all documents; no document is its own partner.
All inputs are finite; a program needn't handle non-finite values.
Results may differ from a plain program's by a relative error of at most 0.005.
Values may be sent and summed in bfloat16 or wider, within the bound.
A program may use at most 128 MiB of HBM per device.

v0:
```python
import jax
import jax.numpy as jnp
from jax import lax
from jax.sharding import PartitionSpec as P


def shards(tokens, factor_one, factor_two, gate_gain, gate_bias, block_counts, partner, reading):
    doc_dev, tok_dev, chan = tokens.shape
    blocks_dev, blk_size = (factor_one.shape[0], factor_one.shape[1])
    all_blocks = factor_two.shape[1]
    all_docs = block_counts.shape[0]
    doc_start = lax.axis_index("doc") * doc_dev
    block_start = lax.axis_index("seq") * blocks_dev
    local_counts = lax.dynamic_slice_in_dim(block_counts, doc_start, doc_dev)
    block_ids = block_start + jnp.arange(blocks_dev, dtype=jnp.int32)
    inside = (block_ids[None, :] < local_counts[:, None]).astype(jnp.bfloat16)
    grid = tokens.reshape(doc_dev, blocks_dev, blk_size, chan) * inside[:, :, None, None]
    mixed = jnp.einsum(
        "dbic,bij->dbjc", grid, factor_one, preferred_element_type=jnp.float32
    ).astype(jnp.bfloat16)
    values_t, inputs_t = (
        lax.all_to_all(mixed, "seq", split_axis=2, concat_axis=1, tiled=True),
        lax.all_to_all(grid, "seq", split_axis=2, concat_axis=1, tiled=True),
    )
    second = jnp.einsum("dpjc,jpq->dqjc", values_t, factor_two, preferred_element_type=jnp.float32)
    gate = jax.nn.sigmoid(gate_gain * inputs_t.astype(jnp.float32) + gate_bias)
    full = second * gate
    gated = full.astype(jnp.bfloat16)
    row_ids = jnp.arange(all_blocks, dtype=jnp.int32)
    keep = (row_ids[None, :] < local_counts[:, None]).astype(jnp.float32)
    partial_value = jnp.sum(full * keep[:, :, None, None], axis=(1, 2))
    scale_local = 1.0 / jnp.sqrt(local_counts.astype(jnp.float32) * blk_size)
    mine = lax.psum(partial_value, "seq") * scale_local[:, None]
    pooled_all = lax.all_gather(mine, "doc", axis=0, tiled=True)
    local_partner = lax.dynamic_slice_in_dim(partner, doc_start, doc_dev)
    picker = (local_partner[:, None] == jnp.arange(all_docs, dtype=jnp.int32)[None, :]).astype(
        jnp.float32
    )
    other = jnp.dot(picker, pooled_all, precision=lax.Precision.HIGHEST)
    contrast = jnp.dot(mine - other, reading, precision=lax.Precision.HIGHEST)
    return (gated, contrast)


def solution(mesh):
    placed = (
        P("doc", "seq", None),
        P("seq", None, None),
        P("seq", None, None),
        P(),
        P(),
        P(),
        P(),
        P(),
    )
    return jax.shard_map(
        shards,
        mesh=mesh,
        in_specs=placed,
        out_specs=(P("doc", None, "seq", None), P("doc", None)),
        check_vma=False,
    )
```

profile of v0, /device:TPU:0, one launch (start us, length us, event | category | flops | bytes accessed | tf_op | source)
XLA Modules:
  0.0 254.0 jit_solution(281498161123050045)
XLA Ops:
  0.6 0.0 copy-start
  0.7 0.9 multiply_rsqrt_fusion
  1.5 7.5 %fusion.21 = bf16[4,1,1024,512]{3,0,1,2:T(4,128)(2,1)} fusion(bf16[4]{0:T(256)(128)(2,1)S(1)} %compare_convert_fusion, bf16[4,1024,512]{2,1,0:T(8,128)(2,1)} %param.8), kind=kLoop, calls=%fused_computation.24 | loop fusion | flops 2097152 | bytes 8388616 | tf_op jit(solution)/shard_map/mul | solution.py:17
  9.0 7.3 %all-to-all-start.1 = ((bf16[4,1,1024,512]{3,0,1,2:T(4,128)(2,1)}), bf16[4,1,1024,512]{3,0,1,2:T(4,128)(2,1)}, u32[]{:S(2)}, u32[]{:S(2)}) async-start(bf16[4,1,1024,512]{3,0,1,2:T(4,128)(2,1)} %fusion.21), calls=%async_computation.1 | async-start | bytes 8388608 | tf_op jit(solution)/shard_map/all_to_all | solution.py:23
  16.2 5.4 %copy_multiply_fusion.1 = bf16[4,1024,512]{2,0,1:T(4,128)(2,1)S(1)} fusion(bf16[4,1024,512]{2,1,0:T(8,128)(2,1)} %param.8, bf16[4]{0:T(256)(128)(2,1)S(1)} %compare_convert_fusion), kind=kLoop, calls=%fused_computation.12 | loop fusion | flops 2097152 | bytes 8388616 | tf_op jit(solution)/shard_map/mul | solution.py:17
  21.7 6.5 %convert_bitcast_fusion = bf16[4,1,1024,512]{2,3,0,1:T(8,128)(2,1)} fusion(bf16[4,1024,512]{2,0,1:T(4,128)(2,1)S(1)} %copy_multiply_fusion.1, bf16[1,1024,1024]{2,1,0:T(8,128)(2,1)S(1)} %copy-done), kind=kOutput, calls=%fused_computation.13 | convolution fusion | flops 4297064448 | bytes 10485760 | tf_op jit(solution)/shard_map/dbic,bij->dbjc/dot_general | solution.py:18
  28.2 7.9 %copy.28 = bf16[4,1,1024,512]{3,0,1,2:T(4,128)(2,1)} copy(bf16[4,1,1024,512]{2,3,0,1:T(8,128)(2,1)} %convert_bitcast_fusion) | data formatting | bytes 8388608 | tf_op jit(solution)/shard_map/convert_element_type | solution.py:20
  36.0 73.5 %all-to-all-done.1 = bf16[4,1,1024,512]{3,0,1,2:T(4,128)(2,1)} async-done(((bf16[4,1,1024,512]{3,0,1,2:T(4,128)(2,1)}), bf16[4,1,1024,512]{3,0,1,2:T(4,128)(2,1)}, u32[]{:S(2)}, u32[]{:S(2)}) %all-to-all-start.1) | async-done | bytes 4194336 | tf_op jit(solution)/shard_map/all_to_all | solution.py:23
  109.5 4.8 %all-to-all-start = ((bf16[4,1,1024,512]{3,0,1,2:T(4,128)(2,1)}), bf16[4,1,1024,512]{3,0,1,2:T(4,128)(2,1)}, u32[]{:S(2)}, u32[]{:S(2)}) async-start(bf16[4,1,1024,512]{3,0,1,2:T(4,128)(2,1)} %copy.28), calls=%async_computation | async-start | bytes 8388608 | tf_op jit(solution)/shard_map/all_to_all | solution.py:22
  114.3 0.1 dynamic_slice.7
  114.4 0.2 copy.35
  114.6 0.1 fusion.14
  114.7 3.0 %copy.32 = bf16[4,1,1024,512]{3,2,0,1:T(8,128)(2,1)S(1)} copy(bf16[4,1,1024,512]{3,0,1,2:T(4,128)(2,1)} %all-to-all-done.1) | data formatting | bytes 8388608 | tf_op jit(solution)/shard_map/all_to_all | solution.py:23
  117.7 0.0 copy-start.3
  117.7 0.0 copy-start.4
  117.7 4.4 %convert.1 = f32[4,8,128,512]{3,2,1,0:T(8,128)} convert(bf16[4,8,128,512]{3,2,1,0:T(8,128)(2,1)S(1)} %bitcast.24) | non-fusion elementwise | flops 2097152 | bytes 12582912 | tf_op jit(solution)/shard_map/convert_element_type | solution.py:26
  122.1 84.6 %all-to-all-done = bf16[4,1,1024,512]{3,0,1,2:T(4,128)(2,1)} async-done(((bf16[4,1,1024,512]{3,0,1,2:T(4,128)(2,1)}), bf16[4,1,1024,512]{3,0,1,2:T(4,128)(2,1)}, u32[]{:S(2)}, u32[]{:S(2)}) %all-to-all-start) | async-done | bytes 4194336 | tf_op jit(solution)/shard_map/all_to_all | solution.py:22
  206.7 14.7 %multiply_reduce_fusion = (f32[4,512]{1,0:T(4,128)S(1)}, bf16[4,8,128,512]{3,1,0,2:T(8,128)(2,1)}) fusion(f32[4,8]{1,0:T(4,128)S(1)} %fusion.14, f32[512]{0:T(512)S(1)} %copy-done.3, f32[4,8,128,512]{3,2,1,0:T(8,128)} %convert.1, f32[512]{0:T(512)S(1)} %copy-done.4, bf16[128,8,8,1]{1,2,3,0:T(8,128)(2,1)S(1)} %copy.35, bf16[4,8,128,512]{3,0,2,1:T(4,128)(2,1)} %bitcast.5), kind=kOutput, calls=%fused_computation.7 | convolution fusion | flops 52426752 | bytes 16806016 | tf_op jit(solution)/shard_map/dpjc,jpq->dqjc/dot_general | solution.py:25
  221.4 19.6 %psum.7 = f32[4,512]{1,0:T(4,128)S(1)} all-reduce(f32[4,512]{1,0:T(4,128)S(1)} %get-tuple-element.12), channel_id=1, replica_groups=mesh['seq'=8,'doc'=4] {'seq'}, use_global_device_ids=true, to_apply=%region_1.0 | all-reduce | flops 2048 | bytes 16384 | tf_op jit(solution)/shard_map/psum | solution.py:33
  241.0 0.1 multiply_bitcast_fusion
  241.1 5.2 %all-gather = f32[4,4,512]{2,1,0:T(4,128)S(1)} all-gather(f32[1,4,512]{2,1,0:T(4,128)S(1)} %multiply_bitcast_fusion), channel_id=1, replica_groups=mesh['seq'=8,'doc'=4] {'doc'}, dimensions={0}, use_global_device_ids=true | all-gather | bytes 40960 | tf_op jit(solution)/shard_map/all_gather | solution.py:34
  246.3 6.6 %copy.34 = bf16[4,8,128,512]{3,2,1,0:T(8,128)(2,1)} copy(bf16[4,8,128,512]{3,1,0,2:T(8,128)(2,1)} %get-tuple-element.13) | data formatting | bytes 8388608
  252.9 0.2 convolution_subtract_fusion
  253.1 0.9 fusion.16
  (11 shorter events, 0.0 us)
Async XLA Ops:
  0.6 21.1 %copy-start = (bf16[1,1024,1024]{2,1,0:T(8,128)(2,1)S(1)}, bf16[1,1024,1024]{2,1,0:T(8,128)(2,1)}, u32[]{:S(2)}) copy-start(bf16[1,1024,1024]{2,1,0:T(8,128)(2,1)} %param.9) | copy-start | bytes 6291460
  9.0 100.5 %all-to-all-start.1 = ((bf16[4,1,1024,512]{3,0,1,2:T(4,128)(2,1)}), bf16[4,1,1024,512]{3,0,1,2:T(4,128)(2,1)}, u32[]{:S(2)}, u32[]{:S(2)}) async-start(bf16[4,1,1024,512]{3,0,1,2:T(4,128)(2,1)} %fusion.21), calls=%async_computation.1 | async-start | bytes 8388608 | tf_op jit(solution)/shard_map/all_to_all | solution.py:23
  36.0 78.3 %copy-start.5 = (s32[16]{0:T(128)S(1)}, s32[16]{0:T(128)}, u32[]{:S(2)}) copy-start(s32[16]{0:T(128)} %param.14) | copy-start | bytes 196
  36.0 78.4 %copy-start.2 = (bf16[128,8,8]{0,2,1:T(8,128)(2,1)S(1)}, bf16[128,8,8]{0,2,1:T(8,128)(2,1)}, u32[]{:S(2)}) copy-start(bf16[128,8,8]{0,2,1:T(8,128)(2,1)} %param.10) | copy-start | bytes 49156
  109.5 97.2 %all-to-all-start = ((bf16[4,1,1024,512]{3,0,1,2:T(4,128)(2,1)}), bf16[4,1,1024,512]{3,0,1,2:T(4,128)(2,1)}, u32[]{:S(2)}, u32[]{:S(2)}) async-start(bf16[4,1,1024,512]{3,0,1,2:T(4,128)(2,1)} %copy.28), calls=%async_computation | async-start | bytes 8388608 | tf_op jit(solution)/shard_map/all_to_all | solution.py:22
  117.7 89.0 %copy-start.3 = (f32[512]{0:T(512)S(1)}, f32[512]{0:T(512)}, u32[]{:S(2)}) copy-start(f32[512]{0:T(512)} %param.12) | copy-start | bytes 6148
  117.7 89.0 %copy-start.4 = (f32[512]{0:T(512)S(1)}, f32[512]{0:T(512)}, u32[]{:S(2)}) copy-start(f32[512]{0:T(512)} %param.11) | copy-start | bytes 6148
  246.3 6.8 %copy-start.1 = (f32[512,256]{1,0:T(8,128)S(1)}, f32[512,256]{1,0:T(8,128)}, u32[]{:S(2)}) copy-start(f32[512,256]{1,0:T(8,128)} %param.15) | copy-start | bytes 1572868
where the time goes:
time: 255 us; the launch traced here: 254 us
  waiting for transfers between devices  158 us (62%)
  blocking collectives  24.8 us (10%)
  matrix products  22.2 us (9%)
  other arithmetic  18.3 us (7%)
  local copies, waits for them, and re-layouts  17.8 us (7%)
  starting transfers between devices  12 us (5%)
    all_to_all x1, waiting for transfers between devices, shards(): lax.all_to_all(mixed, 'seq', split_axis=2, concat_axis=1, tiled=True)  84.6 us
    all_to_all x1, waiting for transfers between devices, shards(): lax.all_to_all(grid, 'seq', split_axis=2, concat_axis=1, tiled=True)  73.5 us
    psum x1, blocking collectives, shards(): mine = lax.psum(partial_value, 'seq') * scale_local[:, None]  19.6 us
    dot_general x1, matrix products, shards(): jnp.einsum('dpjc,jpq->dqjc', values_t, factor_two, preferred_element_type...  14.7 us
    mul x2, other arithmetic, shards(): tokens.reshape(doc_dev, blocks_dev, blk_size, chan)  12.9 us
    convert_element_type x1, local copies, waits for them, and re-layouts, shards(): mixed = jnp.einsum('dbic,bij->dbjc', grid, factor_one, preferred_element_...  7.88 us
    all_to_all x1, starting transfers between devices, shards(): lax.all_to_all(grid, 'seq', split_axis=2, concat_axis=1, tiled=True)  7.25 us
    unnamed x15, local copies, waits for them, and re-layouts  6.85 us
  transfers between devices with their start and end apart: 2, of which 2 were waited for; matrix products, arithmetic and copies ran while one was open for 11% of the time, Pallas kernels for 0%

commit v1 on v0

--- a/solution.py
+++ b/solution.py
@@ -2,6 +2,13 @@
 import jax.numpy as jnp
 from jax import lax
 from jax.sharding import PartitionSpec as P
+
+
+def exchange_blocks(array, mesh_axis, split, join):
+    size = lax.axis_size(mesh_axis)
+    blocks = jnp.stack(jnp.split(array, size, axis=split), axis=0)
+    blocks = lax.all_to_all(blocks, mesh_axis, split_axis=0, concat_axis=0)
+    return jnp.concatenate(blocks, axis=join)
 
 
 def shards(tokens, factor_one, factor_two, gate_gain, gate_bias, block_counts, partner, reading):
@@ -19,7 +26,7 @@
         "dbic,bij->dbjc", grid, factor_one, preferred_element_type=jnp.float32
     ).astype(jnp.bfloat16)
     values_t, inputs_t = (
-        lax.all_to_all(mixed, "seq", split_axis=2, concat_axis=1, tiled=True),
+        exchange_blocks(mixed, "seq", 2, 1),
         lax.all_to_all(grid, "seq", split_axis=2, concat_axis=1, tiled=True),
     )
     second = jnp.einsum("dpjc,jpq->dqjc", values_t, factor_two, preferred_element_type=jnp.float32)

time: 255 us -> 263 us (1.031)
  waiting for transfers between devices: 158 us -> 170 us
  matrix products: 22.2 us -> 13.3 us
  local copies, waits for them, and re-layouts: 17.8 us -> 26.4 us
  other arithmetic: 18.3 us -> 15.1 us
    all_to_all x1, waiting for transfers between devices: 73.5 us -> 84.2 us  [shards(): lax.all_to_all(grid, 'seq', split_axis=2, concat_axis=1, tiled=True)]
    reshape x0 -> x1, local copies, waits for them, and re-layouts: none -> 7.89 us  [exchange_blocks(): return jnp.concatenate(blocks, axis=join)]
    convert_element_type x1 -> x0, local copies, waits for them, and re-layouts: 7.88 us -> none  [shards(): mixed = jnp.einsum('dbic,bij->dbjc', grid, factor_one, preferred_element_...]
    dot_general x1, matrix products: 14.7 us -> 7.04 us  [shards(): jnp.einsum('dpjc,jpq->dqjc', values_t, factor_two, preferred_element_type...]
    unnamed x15 -> x24, local copies, waits for them, and re-layouts: 6.85 us -> 14.4 us
    convert_element_type x1, other arithmetic: 4.37 us -> 1.13 us  [shards(): gate = jax.nn.sigmoid(gate_gain * inputs_t.astype(jnp.float32) + gate_bias)]
  transfers between devices with their start and end apart: 2 -> 2, of which waited for: 2 -> 2; matrix products, arithmetic and copies ran while one was open for 11% -> 6% of each run, Pallas kernels for 0% -> 0%
where the time goes in v1:
time: 263 us; the launch traced here: 262 us
  waiting for transfers between devices  170 us (65%)
  local copies, waits for them, and re-layouts  26.4 us (10%)
  blocking collectives  24.8 us (9%)
  other arithmetic  15.1 us (6%)
  matrix products  13.3 us (5%)
  starting transfers between devices  12 us (5%)
    all_to_all x1, waiting for transfers between devices, exchange_blocks(): blocks = lax.all_to_all(blocks, mesh_axis, split_axis=0, concat_axis=0)  85.8 us
    all_to_all x1, waiting for transfers between devices, shards(): lax.all_to_all(grid, 'seq', split_axis=2, concat_axis=1, tiled=True)  84.2 us
    psum x1, blocking collectives, shards(): mine = lax.psum(partial_value, 'seq') * scale_local[:, None]  19.6 us
    unnamed x24, local copies, waits for them, and re-layouts  14.4 us
    mul x2, other arithmetic, shards(): tokens.reshape(doc_dev, blocks_dev, blk_size, chan)  12.9 us
    reshape x1, local copies, waits for them, and re-layouts, exchange_blocks(): return jnp.concatenate(blocks, axis=join)  7.89 us
    all_to_all x1, starting transfers between devices, exchange_blocks(): blocks = lax.all_to_all(blocks, mesh_axis, split_axis=0, concat_axis=0)  7.25 us
    dot_general x1, matrix products, shards(): jnp.einsum('dpjc,jpq->dqjc', values_t, factor_two, preferred_element_type...  7.04 us
  transfers between devices with their start and end apart: 2, of which 2 were waited for; matrix products, arithmetic and copies ran while one was open for 6% of the time, Pallas kernels for 0%

profile of v1, /device:TPU:0, one launch (start us, length us, event | category | flops | bytes accessed | tf_op | source)
XLA Modules:
  0.0 262.3 jit_solution(7599133529356304003)
XLA Ops:
  1.5 5.4 %copy_multiply_fusion.1 = bf16[4,1024,512]{2,0,1:T(4,128)(2,1)S(1)} fusion(bf16[4,1024,512]{2,1,0:T(8,128)(2,1)} %param.8, bf16[4]{0:T(256)(128)(2,1)S(1)} %compare_convert_fusion), kind=kLoop, calls=%fused_computation.10 | loop fusion | flops 2097152 | bytes 8388616 | tf_op jit(solution)/shard_map/mul | solution.py:24
  7.0 5.2 %convert_bitcast_fusion = bf16[4,1,1024,512]{2,3,0,1:T(8,128)(2,1)S(1)} fusion(bf16[4,1024,512]{2,0,1:T(4,128)(2,1)S(1)} %copy_multiply_fusion.1, bf16[1,1024,1024]{2,1,0:T(8,128)(2,1)S(1)} %copy-done), kind=kOutput, calls=%fused_computation.11 | convolution fusion | flops 4297064448 | bytes 10485760 | tf_op jit(solution)/shard_map/dbic,bij->dbjc/dot_general | solution.py:25
  12.2 0.9 fusion.17
  13.1 0.9 fusion.16
  14.0 0.9 fusion.15
  15.0 0.9 fusion.14
  15.9 0.9 fusion.13
  16.9 0.9 fusion.12
  17.8 0.9 fusion.11
  18.7 1.0 fusion.10
  19.7 7.2 %all-to-all-start = ((bf16[8,4,1,128,512]{3,4,1,2,0:T(8,128)(2,1)}), bf16[8,4,1,128,512]{3,4,1,2,0:T(8,128)(2,1)}, u32[]{:S(2)}, u32[]{:S(2)}) async-start(bf16[8,4,1,128,512]{3,4,1,2,0:T(8,128)(2,1)} %fusion.10), calls=%async_computation | async-start | bytes 8388608 | tf_op jit(solution)/shard_map/all_to_all | solution.py:10
  26.9 7.5 %fusion.26 = bf16[4,1,1024,512]{3,0,1,2:T(4,128)(2,1)} fusion(bf16[4]{0:T(256)(128)(2,1)S(1)} %compare_convert_fusion, bf16[4,1024,512]{2,1,0:T(8,128)(2,1)} %param.8), kind=kLoop, calls=%fused_computation.38 | loop fusion | flops 2097152 | bytes 8388616 | tf_op jit(solution)/shard_map/mul | solution.py:24
  34.4 85.8 %all-to-all-done = bf16[8,4,1,128,512]{3,4,1,2,0:T(8,128)(2,1)} async-done(((bf16[8,4,1,128,512]{3,4,1,2,0:T(8,128)(2,1)}), bf16[8,4,1,128,512]{3,4,1,2,0:T(8,128)(2,1)}, u32[]{:S(2)}, u32[]{:S(2)}) %all-to-all-start) | async-done | bytes 4194336 | tf_op jit(solution)/shard_map/all_to_all | solution.py:10
  120.2 4.7 %all-to-all-start.1 = ((bf16[4,1,1024,512]{3,0,1,2:T(4,128)(2,1)}), bf16[4,1,1024,512]{3,0,1,2:T(4,128)(2,1)}, u32[]{:S(2)}, u32[]{:S(2)}) async-start(bf16[4,1,1024,512]{3,0,1,2:T(4,128)(2,1)} %fusion.26), calls=%async_computation.1 | async-start | bytes 8388608 | tf_op jit(solution)/shard_map/all_to_all | solution.py:30
  125.3 7.9 %copy.21 = bf16[4,8,128,512]{3,1,0,2:T(8,128)(2,1)} copy(bf16[4,8,128,512]{2,3,0,1:T(8,128)(2,1)} %bitcast.16) | data formatting | bytes 8388608 | tf_op jit(solution)/shard_map/reshape | solution.py:11
  133.2 84.2 %all-to-all-done.1 = bf16[4,1,1024,512]{3,0,1,2:T(4,128)(2,1)} async-done(((bf16[4,1,1024,512]{3,0,1,2:T(4,128)(2,1)}), bf16[4,1,1024,512]{3,0,1,2:T(4,128)(2,1)}, u32[]{:S(2)}, u32[]{:S(2)}) %all-to-all-start.1) | async-done | bytes 4194336 | tf_op jit(solution)/shard_map/all_to_all | solution.py:30
  217.4 3.0 %copy.23 = bf16[4,1,1024,512]{3,2,0,1:T(8,128)(2,1)S(1)} copy(bf16[4,1,1024,512]{3,0,1,2:T(4,128)(2,1)} %all-to-all-done.1) | data formatting | bytes 8388608 | tf_op jit(solution)/shard_map/all_to_all | solution.py:30
  220.5 1.1 convert.1
  221.6 1.0 copy-done.1
  222.6 7.0 %multiply_reduce_fusion = (f32[4,512]{1,0:T(4,128)S(1)}, bf16[4,8,128,512]{3,1,0,2:T(8,128)(2,1)}) fusion(f32[4,8]{1,0:T(4,128)S(1)} %fusion.18, f32[512]{0:T(512)S(1)} %copy-done.4, f32[4,8,128,512]{3,2,1,0:T(8,128)S(1)} %convert.1, f32[512]{0:T(512)S(1)} %copy-done.5, bf16[4,8,128,512]{3,1,0,2:T(8,128)(2,1)S(1)} %copy-done.1, ...), kind=kOutput, calls=%fused_computation.7 | convolution fusion | flops 52426752 | bytes 16806016 | tf_op jit(solution)/shard_map/dpjc,jpq->dqjc/dot_general | solution.py:32
  229.7 19.6 %psum.7 = f32[4,512]{1,0:T(4,128)S(1)} all-reduce(f32[4,512]{1,0:T(4,128)S(1)} %get-tuple-element.10), channel_id=1, replica_groups=mesh['seq'=8,'doc'=4] {'seq'}, use_global_device_ids=true, to_apply=%region_1.0 | all-reduce | flops 2048 | bytes 16384 | tf_op jit(solution)/shard_map/psum | solution.py:40
  249.4 5.2 %all-gather = f32[4,4,512]{2,1,0:T(4,128)S(1)} all-gather(f32[1,4,512]{2,1,0:T(4,128)S(1)} %multiply_bitcast_fusion), channel_id=1, replica_groups=mesh['seq'=8,'doc'=4] {'doc'}, dimensions={0}, use_global_device_ids=true | all-gather | bytes 40960 | tf_op jit(solution)/shard_map/all_gather | solution.py:41
  254.6 6.6 %copy.25 = bf16[4,8,128,512]{3,2,1,0:T(8,128)(2,1)} copy(bf16[4,8,128,512]{3,1,0,2:T(8,128)(2,1)} %get-tuple-element.11) | data formatting | bytes 8388608
  261.4 0.9 fusion.20
  (21 shorter events, 1.6 us)
Async XLA Ops:
  0.6 6.4 %copy-start = (bf16[1,1024,1024]{2,1,0:T(8,128)(2,1)S(1)}, bf16[1,1024,1024]{2,1,0:T(8,128)(2,1)}, u32[]{:S(2)}) copy-start(bf16[1,1024,1024]{2,1,0:T(8,128)(2,1)} %param.9) | copy-start | bytes 6291460
  19.7 100.5 %all-to-all-start = ((bf16[8,4,1,128,512]{3,4,1,2,0:T(8,128)(2,1)}), bf16[8,4,1,128,512]{3,4,1,2,0:T(8,128)(2,1)}, u32[]{:S(2)}, u32[]{:S(2)}) async-start(bf16[8,4,1,128,512]{3,4,1,2,0:T(8,128)(2,1)} %fusion.10), calls=%async_computation | async-start | bytes 8388608 | tf_op jit(solution)/shard_map/all_to_all | solution.py:10
  34.4 90.6 %copy-start.6 = (s32[16]{0:T(128)S(1)}, s32[16]{0:T(128)}, u32[]{:S(2)}) copy-start(s32[16]{0:T(128)} %param.14) | copy-start | bytes 196
  34.4 90.7 %copy-start.3 = (bf16[128,8,8]{0,2,1:T(8,128)(2,1)S(1)}, bf16[128,8,8]{0,2,1:T(8,128)(2,1)}, u32[]{:S(2)}) copy-start(bf16[128,8,8]{0,2,1:T(8,128)(2,1)} %param.10) | copy-start | bytes 49156
  120.2 97.2 %all-to-all-start.1 = ((bf16[4,1,1024,512]{3,0,1,2:T(4,128)(2,1)}), bf16[4,1,1024,512]{3,0,1,2:T(4,128)(2,1)}, u32[]{:S(2)}, u32[]{:S(2)}) async-start(bf16[4,1,1024,512]{3,0,1,2:T(4,128)(2,1)} %fusion.26), calls=%async_computation.1 | async-start | bytes 8388608 | tf_op jit(solution)/shard_map/all_to_all | solution.py:30
  220.4 2.2 copy-start.1
  220.4 2.2 copy-start.4
  220.5 2.2 copy-start.5
  254.6 6.8 %copy-start.2 = (f32[512,256]{1,0:T(8,128)S(1)}, f32[512,256]{1,0:T(8,128)}, u32[]{:S(2)}) copy-start(f32[512,256]{1,0:T(8,128)} %param.15) | copy-start | bytes 1572868
